TPU v7x, 32 devices: a whole 2x2x4 slice. The times are simulated.
32 devices in a mesh: dp: 16 (over z, y, x), rep: 2 (over core).
Axes of the slice: x: 2, y: 2, z: 4, core: 2. Of those that a mesh axis runs over, the one named last changes fastest.
Arguments:
- table: float32 [131072, 400], P(('dp', 'rep')), may hold values from -6 to 6
- batch_index: int32 [32768], P(('dp', 'rep')), may hold values from 0 to 4095
- labels: int32 [32768], P(('dp', 'rep')), may hold values from 0 to 46
- w_branch: float32 [4, 100, 512], P(None, None, 'dp'), may hold values from -0.625 to 0.625
- w_merge: float32 [2048, 512], P('dp'), may hold values from -0.125 to 0.125
- w_class: float32 [512, 47], P('dp'), may hold values from -0.5 to 0.5
- small_params: float32 [20, 512], P(None, 'dp'), as said below
- first_branch: float32 [4, 100, 512], P(None, None, 'dp'), may hold values from -0.0014648438 to 0.0014648438
- first_merge: float32 [2048, 512], P('dp'), may hold values from -0.0014648438 to 0.0014648438
- first_class: float32 [512, 47], P('dp'), may hold values from -0.0014648438 to 0.0014648438
- first_small: float32 [20, 512], P(None, 'dp'), may hold values from -0.00390625 to 0.00390625
- second_branch: float32 [4, 100, 512], P(None, None, 'dp'), may hold values from 7.7659046e-10 to 3.1063618e-09
- second_merge: float32 [2048, 512], P('dp'), may hold values from 7.7659046e-10 to 3.1063618e-09
- second_class: float32 [512, 47], P('dp'), may hold values from 7.7659046e-10 to 3.1063618e-09
- second_small: float32 [20, 512], P(None, 'dp'), may hold values from 6.989314e-09 to 2.7957256e-08
Outputs:
- new_branch: float32 [4, 100, 512], P(None, None, 'dp')
- new_merge: float32 [2048, 512], P('dp')
- new_class: float32 [512, 47], P('dp')
- new_small: float32 [20, 512], P(None, 'dp')
- moment_branch: float32 [4, 100, 512], P(None, None, 'dp')
- moment_merge: float32 [2048, 512], P('dp')
- moment_class: float32 [512, 47], P('dp')
- moment_small: float32 [20, 512], P(None, 'dp')
- square_branch: float32 [4, 100, 512], P(None, None, 'dp')
- square_merge: float32 [2048, 512], P('dp')
- square_class: float32 [512, 47], P('dp')
- square_small: float32 [20, 512], P(None, 'dp')
- copy_branch: bfloat16 [4, 100, 512], P(None, None, 'dp')
- copy_merge: bfloat16 [2048, 512], P('dp')
- copy_class: bfloat16 [512, 47], P('dp')
- copy_small: bfloat16 [20, 512], P(None, 'dp')
- grad_norm: float32 [], replicated
- row_grads: float32 [32768, 400], P(('dp', 'rep'))
Inputs may be any that keep to these rules, and one draw needn't show every extreme that they name: `batch_index`: each entry indexes a row of the block of 4096 table rows that lies on the same device as the entry. `small_params`: gains lie in 0.3 to 2.0, slopes in 0.05 to 0.45.
All inputs are finite; a program needn't handle non-finite values.
Results may differ from a plain program's by a relative error of at most 0.011.
Values may be sent and summed in bfloat16 or wider, within the bound.
No kernel may reach another device: no remote copies, remote signals or barrier semaphores. Data moves between devices by JAX's collectives and lax.ppermute only.
A program may use at most 128 MiB of HBM per device.

v0:
```python
import jax
import jax.numpy as jnp
from jax import lax
from jax.sharding import PartitionSpec as P

HOPS = 4
STEP = 7
EPS_NORM = 1e-05


def leaky(value, slope):
    return slope * value + (1.0 - slope) * value * jax.nn.sigmoid(value)


def leaky_back(upstream, value, slope):
    sig = jax.nn.sigmoid(value)
    slope_term = jnp.sum(upstream * value * (1.0 - sig), axis=0)
    derivative = slope + (1.0 - slope) * (sig + value * sig * (1.0 - sig))
    return (upstream * derivative, slope_term)


def cross_dot(left, right):
    return lax.dot_general(
        left, right, (((0,), (0,)), ((), ())), preferred_element_type=jnp.float32
    )


def back_dot(left, right):
    return lax.dot_general(
        left, right, (((1,), (1,)), ((), ())), preferred_element_type=jnp.float32
    )


def adamw(weight, grad, moment, square, scale, rate):
    clipped = grad * scale
    moment_new = 0.9 * moment + 0.1 * clipped
    square_new = 0.999 * square + 0.001 * clipped * clipped
    fix_one = 1.0 - 0.9**STEP
    fix_two = 1.0 - 0.999**STEP
    update = moment_new / fix_one / (jnp.sqrt(square_new / fix_two) + 1e-08) + 0.01 * weight
    weight_new = weight - rate * update
    return (weight_new, moment_new, square_new)


def on_device(
    table,
    batch_index,
    labels,
    w_branch,
    w_merge,
    w_class,
    small_params,
    first_branch,
    first_merge,
    first_class,
    first_small,
    second_branch,
    second_merge,
    second_class,
    second_small,
):
    batch = batch_index.shape[0]
    row_count = batch * lax.axis_size("dp") * lax.axis_size("rep")
    d_in = w_branch.shape[1]
    hidden = w_merge.shape[1]
    hidden_width = HOPS * hidden
    classes = w_class.shape[1]
    rows = jnp.take(table, batch_index, axis=0)
    input_features = rows.astype(jnp.bfloat16).reshape(batch, HOPS, d_in)
    branch_full, merge_full, class_full, small_full = (
        lax.all_gather(w_branch.astype(jnp.bfloat16), "dp", axis=2, tiled=True),
        lax.all_gather(w_merge.astype(jnp.bfloat16), "dp", axis=0, tiled=True),
        lax.all_gather(w_class.astype(jnp.bfloat16), "dp", axis=0, tiled=True),
        lax.all_gather(small_params.astype(jnp.bfloat16), "dp", axis=1, tiled=True),
    )
    params = small_full.astype(jnp.float32)
    gain1 = params[0:HOPS].reshape(hidden_width)
    shift1 = params[HOPS : 2 * HOPS].reshape(hidden_width)
    slope1 = params[2 * HOPS : 3 * HOPS].reshape(hidden_width)
    slope_join = params[3 * HOPS : 4 * HOPS].reshape(hidden_width)
    gain2 = params[4 * HOPS]
    shift2 = params[4 * HOPS + 1]
    slope2 = params[4 * HOPS + 2]
    bias3 = params[4 * HOPS + 3, :classes]
    first_pre = jnp.einsum(
        "fsq,sqv->fsv", input_features, branch_full, preferred_element_type=jnp.float32
    ).reshape(batch, hidden_width)
    sums_one = lax.psum(
        (jnp.sum(first_pre, axis=0), jnp.sum(first_pre * first_pre, axis=0)), ("dp", "rep")
    )
    mean1 = sums_one[0] / row_count
    inv1 = lax.rsqrt(sums_one[1] / row_count - mean1 * mean1 + EPS_NORM)
    norm1 = (first_pre - mean1) * inv1
    lin1 = gain1 * norm1 + shift1
    act1 = leaky(lin1, slope1)
    joined_low = leaky(act1, slope_join).astype(jnp.bfloat16)
    pre2 = jnp.dot(joined_low, merge_full, preferred_element_type=jnp.float32)
    sums_two = lax.psum((jnp.sum(pre2, axis=0), jnp.sum(pre2 * pre2, axis=0)), ("dp", "rep"))
    mean2 = sums_two[0] / row_count
    inv2 = lax.rsqrt(sums_two[1] / row_count - mean2 * mean2 + EPS_NORM)
    norm2 = (pre2 - mean2) * inv2
    lin2 = gain2 * norm2 + shift2
    act2_low = leaky(lin2, slope2).astype(jnp.bfloat16)
    logits = jnp.dot(act2_low, class_full, preferred_element_type=jnp.float32) + bias3
    probs = jax.nn.softmax(logits, axis=1)
    onehot = (labels[:, None] == jnp.arange(classes, dtype=jnp.int32)[None, :]).astype(jnp.float32)
    dlogits = (probs - onehot).astype(jnp.bfloat16)
    branch_back, merge_back, class_back = (
        lax.all_gather(w_branch.astype(jnp.bfloat16), "dp", axis=2, tiled=True),
        lax.all_gather(w_merge.astype(jnp.bfloat16), "dp", axis=0, tiled=True),
        lax.all_gather(w_class.astype(jnp.bfloat16), "dp", axis=0, tiled=True),
    )
    grad_class = cross_dot(act2_low, dlogits)
    grad_bias3 = jnp.sum(dlogits.astype(jnp.float32), axis=0)
    dact2 = back_dot(dlogits, class_back)
    dy2, grad_slope2 = leaky_back(dact2, lin2, slope2)
    gain2_part = jnp.sum(dy2 * norm2, axis=0)
    shift2_part = jnp.sum(dy2, axis=0)
    totals_two = lax.psum((shift2_part, gain2_part), ("dp", "rep"))
    dpre2 = (
        inv2
        * (
            gain2 * dy2
            - gain2 * totals_two[0] / row_count
            - norm2 * gain2 * totals_two[1] / row_count
        )
    ).astype(jnp.bfloat16)
    grad_merge = cross_dot(joined_low, dpre2)
    djoined = back_dot(dpre2, merge_back)
    dact1, grad_slope_join = leaky_back(djoined, act1, slope_join)
    dy1, grad_slope1 = leaky_back(dact1, lin1, slope1)
    gain1_part = jnp.sum(dy1 * norm1, axis=0)
    shift1_part = jnp.sum(dy1, axis=0)
    totals_one = lax.psum((shift1_part, gain1_part), ("dp", "rep"))
    first_grad = (
        inv1
        * (
            gain1 * dy1
            - gain1 * totals_one[0] / row_count
            - norm1 * gain1 * totals_one[1] / row_count
        )
    ).astype(jnp.bfloat16)
    first_grad = first_grad.reshape(batch, HOPS, hidden)
    branch_gradient = jnp.einsum(
        "pze,pzv->zev", input_features, first_grad, preferred_element_type=jnp.float32
    )
    row_grads = jnp.einsum(
        "fsz,sez->fse", first_grad, branch_back, preferred_element_type=jnp.float32
    ).reshape(batch, HOPS * d_in)
    bias_row = jnp.zeros((hidden,), jnp.float32).at[:classes].set(grad_bias3)
    grad_small = jnp.concatenate(
        [
            gain1_part.reshape(HOPS, hidden),
            shift1_part.reshape(HOPS, hidden),
            grad_slope1.reshape(HOPS, hidden),
            grad_slope_join.reshape(HOPS, hidden),
            gain2_part[None],
            shift2_part[None],
            grad_slope2[None],
            bias_row[None],
        ],
        axis=0,
    )
    paired = (
        lax.psum(branch_gradient.astype(jnp.bfloat16), "rep").astype(jnp.float32),
        lax.psum(grad_merge.astype(jnp.bfloat16), "rep").astype(jnp.float32),
        lax.psum(grad_class.astype(jnp.bfloat16), "rep").astype(jnp.float32),
        lax.psum(grad_small.astype(jnp.bfloat16), "rep").astype(jnp.float32),
    )
    shares = (
        lax.psum_scatter(paired[0], "dp", scatter_dimension=2, tiled=True),
        lax.psum_scatter(paired[1], "dp", scatter_dimension=0, tiled=True),
        lax.psum_scatter(paired[2], "dp", scatter_dimension=0, tiled=True),
        lax.psum_scatter(paired[3], "dp", scatter_dimension=1, tiled=True),
    )
    local_squares = jnp.float32(0.0)
    for share in shares:
        local_squares = local_squares + jnp.sum(share * share)
    grad_norm = jnp.sqrt(lax.psum(local_squares, "dp"))
    scale = 1.0 / jnp.maximum(grad_norm, 1.0)
    weights = (w_branch, w_merge, w_class, small_params)
    firsts = (first_branch, first_merge, first_class, first_small)
    seconds = (second_branch, second_merge, second_class, second_small)
    rates = (0.05, 0.05, 0.05, 0.3)
    results = [
        adamw(w, g, m, v, scale, r)
        for w, g, m, v, r in zip(weights, shares, firsts, seconds, rates)
    ]
    news = tuple((r[0] for r in results))
    moments = tuple((r[1] for r in results))
    squares = tuple((r[2] for r in results))
    copies = tuple((r.astype(jnp.bfloat16) for r in news))
    return (
        news[0],
        news[1],
        news[2],
        news[3],
        moments[0],
        moments[1],
        moments[2],
        moments[3],
        squares[0],
        squares[1],
        squares[2],
        squares[3],
        copies[0],
        copies[1],
        copies[2],
        copies[3],
        grad_norm,
        row_grads,
    )


def solution(mesh):
    placed = (
        P(("dp", "rep"), None),
        P(("dp", "rep")),
        P(("dp", "rep")),
        P(None, None, "dp"),
        P("dp", None),
        P("dp", None),
        P(None, "dp"),
        P(None, None, "dp"),
        P("dp", None),
        P("dp", None),
        P(None, "dp"),
        P(None, None, "dp"),
        P("dp", None),
        P("dp", None),
        P(None, "dp"),
    )
    return jax.shard_map(
        on_device,
        mesh=mesh,
        in_specs=placed,
        out_specs=(
            P(None, None, "dp"),
            P("dp", None),
            P("dp", None),
            P(None, "dp"),
            P(None, None, "dp"),
            P("dp", None),
            P("dp", None),
            P(None, "dp"),
            P(None, None, "dp"),
            P("dp", None),
            P("dp", None),
            P(None, "dp"),
            P(None, None, "dp"),
            P("dp", None),
            P("dp", None),
            P(None, "dp"),
            P(),
            P(("dp", "rep"), None),
        ),
        check_vma=False,
    )
```

profile of v0, /device:TPU:0, one launch (start us, length us, event | category | flops | bytes accessed | tf_op | source)
XLA Modules:
  0.0 804.2 jit_solution(16714491165405822003)
XLA Ops:
  12.6 43.0 %all-gather = bf16[16,32,20]{1,2,0:T(8,128)(2,1)S(1)} all-gather(bf16[1,32,20]{1,2,0:T(8,128)(2,1)S(1)} %convert_bitcast_fusion), channel_id=1, replica_groups=mesh['dp'=16,'rep'=2] {'dp'}, dimensions={0}, use_global_device_ids=true | all-gather | bytes 21760 | tf_op jit(solution)/shard_map/all_gather | solution.py:74
  55.8 40.4 %all_gather.15 = bf16[4,100,512]{1,2,0:T(8,128)(2,1)S(1)} all-gather(bf16[4,100,32]{1,2,0:T(8,128)(2,1)S(1)} %convert_element_type.78), channel_id=1, replica_groups=mesh['dp'=16,'rep'=2] {'dp'}, dimensions={2}, use_global_device_ids=true | all-gather | bytes 435200 | tf_op jit(solution)/shard_map/all_gather | solution.py:71
  96.2 6.9 copy.50
  103.1 6.7 gather_fusion
  110.5 4.5 fusion
  115.0 9.2 %copy.53 = f32[1024,2048]{1,0:T(8,128)} copy(f32[1024,2048]{0,1:T(8,128)} %bitcast.71) | data formatting | bytes 16777216 | tf_op jit(solution)/shard_map/reshape | solution.py:87
  124.2 37.0 %all-reduce.4 = (f32[2048]{0:T(1024)S(1)}, f32[2048]{0:T(1024)S(1)}) all-reduce(f32[2048]{0:T(1024)S(1)} %bitcast.97, f32[2048]{0:T(1024)S(1)} %bitcast.96), channel_id=1, replica_groups=mesh['dp'=16,'rep'=2] {'dp','rep'}, use_global_device_ids=true, to_apply=%region_3.4 | all-reduce | flops 4096 | bytes 32768 | tf_op jit(solution)/shard_map/psum | solution.py:88
  161.1 43.3 %all_gather.18 = bf16[512,47]{1,0:T(8,128)(2,1)} all-gather(bf16[32,47]{1,0:T(8,128)(2,1)S(1)} %convert_element_type.84), channel_id=1, replica_groups=mesh['dp'=16,'rep'=2] {'dp'}, dimensions={0}, use_global_device_ids=true | all-gather | bytes 51136 | tf_op jit(solution)/shard_map/all_gather | solution.py:73
  205.5 9.1 %add_convert_fusion = bf16[1024,2048]{1,0:T(8,128)(2,1)} fusion(f32[2048]{0:T(1024)S(1)} %get-tuple-element.89, f32[2048]{0:T(1024)S(1)} %bitcast.86, f32[2048]{0:T(1024)S(1)} %broadcast_subtract_fusion.1, f32[2048]{0:T(1024)S(1)} %bitcast.92, f32[2048]{0:T(1024)S(1)} %get-tuple-element.82, f32[1024,2048]{1,0:T(8,128)} %copy.53, ...), kind=kLoop, calls=%fused_computation.10 | loop fusion | flops 39845888 | bytes 12648448 | tf_op jit(solution)/shard_map/convert_element_type | solution.py:96
  214.7 5.2 multiply_reduce_fusion.5
  219.9 37.1 %all-reduce.3 = (f32[512]{0:T(512)}, f32[512]{0:T(512)}) all-reduce(f32[512]{0:T(512)S(1)} %get-tuple-element.40, f32[512]{0:T(512)S(1)} %get-tuple-element.39), channel_id=1, replica_groups=mesh['dp'=16,'rep'=2] {'dp','rep'}, use_global_device_ids=true, to_apply=%region_7.8 | all-reduce | flops 1024 | bytes 8192 | tf_op jit(solution)/shard_map/psum | solution.py:98
  263.2 4.2 multiply_reduce_fusion.3
  268.6 41.4 %all-reduce.2 = (f32[512]{0:T(512)}, f32[512]{0:T(512)}) all-reduce(f32[512]{0:T(512)} %copy-done.14, f32[512]{0:T(512)} %copy-done.15), channel_id=1, replica_groups=mesh['dp'=16,'rep'=2] {'dp','rep'}, use_global_device_ids=true, to_apply=%region_13.14 | all-reduce | flops 1024 | bytes 8192 | tf_op jit(solution)/shard_map/psum | solution.py:119
  310.9 2.7 multiply_convert_fusion.1
  313.6 3.8 convolution_convert_fusion
  317.4 13.9 %multiply_reduce_fusion = (bf16[2048]{0:T(1024)(128)(2,1)S(1)}, bf16[2048]{0:T(1024)(128)(2,1)S(1)}, f32[2048]{0:T(1024)S(1)}, f32[2048]{0:T(1024)S(1)}, f32[1024,2048]{1,0:T(8,128)}) fusion(f32[2048]{0:T(1024)S(1)} %broadcast_subtract_fusion.1, f32[2048]{0:T(1024)S(1)} %bitcast.93, f32[2048]{0:T(1024)S(1)} %get-tuple-element.82, ...), kind=kOutput, calls=%fused_computation.4 | convolution fusion | flops 2225070080 | bytes 20013056 | tf_op jit(solution)/shard_map/dot_general | solution.py:29
  331.3 40.2 %all-reduce.1 = (f32[2048]{0:T(1024)S(1)}, f32[2048]{0:T(1024)S(1)}) all-reduce(f32[2048]{0:T(1024)S(1)} %get-tuple-element.32, f32[2048]{0:T(1024)S(1)} %get-tuple-element.33), channel_id=1, replica_groups=mesh['dp'=16,'rep'=2] {'dp','rep'}, use_global_device_ids=true, to_apply=%region_17.18 | all-reduce | flops 4096 | bytes 32768 | tf_op jit(solution)/shard_map/psum | solution.py:134
  371.7 1.9 concatenate.6
  373.8 7.3 multiply_convert_fusion
  381.1 1.9 copy-done
  383.0 2.5 fusion.10
  385.6 5.8 all-reduce.10.cloned.1.call-done
  394.8 23.1 %all-reduce.12.cloned.1.call-done = (bf16[4,100,512]{1,2,0:T(8,128)(2,1)}, bf16[2048,512]{1,0:T(8,128)(2,1)}) async-done(((bf16[4,100,512]{1,2,0:T(8,128)(2,1)}, bf16[2048,512]{1,0:T(8,128)(2,1)}), (bf16[4,100,512]{1,2,0:T(8,128)(2,1)}, bf16[2048,512]{1,0:T(8,128)(2,1)})) %all-reduce.12.cloned.1.call-update) | async-done | bytes 2506768 | tf_op jit(solution)/shard_map/psum | solution.py:165
  417.9 2.1 convert_element_type.90
  420.1 4.2 convert_element_type.92
  424.4 3.7 fusion.7
  428.1 69.9 %reduce-scatter.13.cloned.1.call-done = f32[32,20]{1,0:T(8,128)} async-done(((f32[512,20]{1,0:T(8,128)}), f32[32,20]{1,0:T(8,128)}) %reduce-scatter.13.cloned.1.call-update) | async-done | bytes 2576
  499.4 73.8 %reduce-scatter.11.cloned.1.call-done = f32[32,47]{1,0:T(8,128)} async-done(((f32[512,47]{1,0:T(8,128)}), f32[32,47]{1,0:T(8,128)}) %reduce-scatter.11.cloned.1.call-update) | async-done | bytes 6032 | tf_op jit(solution)/shard_map/reduce_scatter | solution.py:173
  574.5 75.5 %reduce-scatter.7.cloned.1.call-done = f32[4,100,32]{1,2,0:T(8,128)} async-done(((f32[4,100,512]{1,2,0:T(8,128)}), f32[4,100,32]{1,2,0:T(8,128)}) %reduce-scatter.7.cloned.1.call-update) | async-done | bytes 51216 | tf_op jit(solution)/shard_map/reduce_scatter | solution.py:171
  651.5 92.4 %reduce-scatter.9.cloned.1.call-done = f32[128,512]{1,0:T(8,128)} async-done(((f32[2048,512]{1,0:T(8,128)}), f32[128,512]{1,0:T(8,128)}) %reduce-scatter.9.cloned.1.call-update) | async-done | bytes 262160 | tf_op jit(solution)/shard_map/reduce_scatter | solution.py:172
  743.9 1.7 multiply_reduce_fusion.6
  749.5 40.5 %psum.103 = f32[]{:T(128)} all-reduce(f32[]{:T(128)S(6)} %add.234), channel_id=1, replica_groups=mesh['dp'=16,'rep'=2] {'dp'}, use_global_device_ids=true, to_apply=%region_34.35 | all-reduce | flops 1 | bytes 8 | tf_op jit(solution)/shard_map/psum | solution.py:179
  (115 shorter events, 30.2 us)
Async XLA Ops:
  7.2 207.5 %all-gather.3.cloned.1.call-start = ((), (), s32[]{:S(2)}) async-start(), calls=%async_computation.4 | async-start | bytes 2228224 | tf_op jit(solution)/shard_map/all_gather | solution.py:72
  8.9 382.5 %all-reduce.10.cloned.1.call-start = ((), (), s32[]{:S(2)}) async-start(), calls=%async_computation.9 | async-start | bytes 311296 | tf_op jit(solution)/shard_map/psum | solution.py:167
  9.6 100.9 %copy-start.16 = (pred[1024]{0:T(1024)(128)(4,1)}, pred[1024]{0:T(1024)(128)(4,1)S(1)}, u32[]{:S(2)}) copy-start(pred[1024]{0:T(1024)(128)(4,1)S(1)} %compare_and_fusion) | copy-start | bytes 3076
  256.9 6.2 copy-start.4
  267.4 0.6 copy-start.14
  267.4 1.1 copy-start.15
  310.0 3.5 copy-start.1
  310.8 6.5 slice-start
  313.5 3.8 slice-start.1
  313.6 3.8 copy-start.21
  317.4 54.2 %copy-start.20 = (bf16[512]{0:T(512)(128)(2,1)S(1)}, bf16[512]{0:T(512)(128)(2,1)}, u32[]{:S(2)}) copy-start(bf16[512]{0:T(512)(128)(2,1)} %get-tuple-element.36) | copy-start | bytes 3076
  317.4 54.2 %copy-start.18 = (bf16[512]{0:T(512)(128)(2,1)S(1)}, bf16[512]{0:T(512)(128)(2,1)}, u32[]{:S(2)}) copy-start(bf16[512]{0:T(512)(128)(2,1)} %convert.38) | copy-start | bytes 3076
  317.4 54.2 %copy-start.19 = (bf16[47]{0:T(256)(128)(2,1)S(1)}, bf16[47]{0:T(256)(128)(2,1)}, u32[]{:S(2)}) copy-start(bf16[47]{0:T(256)(128)(2,1)} %get-tuple-element.69) | copy-start | bytes 286
  373.5 44.4 %all-reduce.12.cloned.1.call-start = ((), (), s32[]{:S(2)}) async-start(), calls=%async_computation.10 | async-start | bytes 5242880 | tf_op jit(solution)/shard_map/psum | solution.py:165
  373.8 9.2 %copy-start.17 = (pred[1024]{0:T(1024)(128)(4,1)S(1)}, pred[1024]{0:T(1024)(128)(4,1)}, u32[]{:S(2)}) copy-start(pred[1024]{0:T(1024)(128)(4,1)} %copy-done.16) | copy-start | bytes 3076
  381.1 1.9 copy-start
  385.5 112.5 %reduce-scatter.13.cloned.1.call-start = ((), (), s32[]{:S(2)}) async-start(), calls=%async_computation.8 | async-start | bytes 278528
  393.0 180.1 %reduce-scatter.11.cloned.1.call-start = ((), (), s32[]{:S(2)}) async-start(), calls=%async_computation.7 | async-start | bytes 278528 | tf_op jit(solution)/shard_map/reduce_scatter | solution.py:173
  394.7 255.3 %reduce-scatter.7.cloned.1.call-start = ((), (), s32[]{:S(2)}) async-start(), calls=%async_computation.5 | async-start | bytes 1114112 | tf_op jit(solution)/shard_map/reduce_scatter | solution.py:171
  420.0 323.9 %reduce-scatter.9.cloned.1.call-start = ((), (), s32[]{:S(2)}) async-start(), calls=%async_computation.6 | async-start | bytes 4456448 | tf_op jit(solution)/shard_map/reduce_scatter | solution.py:172
  424.2 366.6 %copy-start.11 = (f32[20,32]{1,0:T(8,128)S(1)}, f32[20,32]{1,0:T(8,128)}, u32[]{:S(2)}) copy-start(f32[20,32]{1,0:T(8,128)} %param.23) | copy-start | bytes 7684
  424.2 367.9 %copy-start.10 = (f32[32,47]{1,0:T(8,128)S(1)}, f32[32,47]{1,0:T(8,128)}, u32[]{:S(2)}) copy-start(f32[32,47]{1,0:T(8,128)} %param.22) | copy-start | bytes 18052
  424.3 367.9 %copy-start.12 = (f32[32,47]{1,0:T(8,128)S(1)}, f32[32,47]{1,0:T(8,128)}, u32[]{:S(2)}) copy-start(f32[32,47]{1,0:T(8,128)} %param.26) | copy-start | bytes 18052
  424.3 367.9 %copy-start.13 = (f32[32,47]{1,0:T(8,128)S(1)}, f32[32,47]{1,0:T(8,128)}, u32[]{:S(2)}) copy-start(f32[32,47]{1,0:T(8,128)} %param.30) | copy-start | bytes 18052
  424.3 369.3 %copy-start.7 = (f32[4,100,32]{1,2,0:T(8,128)S(1)}, f32[4,100,32]{1,2,0:T(8,128)}, u32[]{:S(2)}) copy-start(f32[4,100,32]{1,2,0:T(8,128)} %param.20) | copy-start | bytes 153604
  424.3 369.2 %copy-start.8 = (f32[4,100,32]{1,2,0:T(8,128)S(1)}, f32[4,100,32]{1,2,0:T(8,128)}, u32[]{:S(2)}) copy-start(f32[4,100,32]{1,2,0:T(8,128)} %param.24) | copy-start | bytes 153604
  424.3 369.2 %copy-start.9 = (f32[4,100,32]{1,2,0:T(8,128)S(1)}, f32[4,100,32]{1,2,0:T(8,128)}, u32[]{:S(2)}) copy-start(f32[4,100,32]{1,2,0:T(8,128)} %param.28) | copy-start | bytes 153604
  424.3 370.8 %copy-start.2 = (f32[128,512]{1,0:T(8,128)S(1)}, f32[128,512]{1,0:T(8,128)}, u32[]{:S(2)}) copy-start(f32[128,512]{1,0:T(8,128)} %param.21) | copy-start | bytes 786436
  424.3 370.8 %copy-start.5 = (f32[128,512]{1,0:T(8,128)S(1)}, f32[128,512]{1,0:T(8,128)}, u32[]{:S(2)}) copy-start(f32[128,512]{1,0:T(8,128)} %param.25) | copy-start | bytes 786436
  424.3 370.8 %copy-start.6 = (f32[128,512]{1,0:T(8,128)S(1)}, f32[128,512]{1,0:T(8,128)}, u32[]{:S(2)}) copy-start(f32[128,512]{1,0:T(8,128)} %param.29) | copy-start | bytes 786436
  743.9 51.2 %copy-start.3 = (f32[128,512]{1,0:T(8,128)S(1)}, f32[128,512]{1,0:T(8,128)}, u32[]{:S(2)}) copy-start(f32[128,512]{1,0:T(8,128)} %reduce-scatter.9.cloned.1.call-done) | copy-start | bytes 786436
Sparse Core Ops, SparseCore 0:
  11.4 66.4 all-gather.2
  373.7 17.7 all-reduce.9
  394.4 23.4 all-reduce.11
  420.7 77.2 reduce-scatter.12
  500.6 72.4 reduce-scatter.10
  575.9 74.0 reduce-scatter.6
  652.3 91.5 reduce-scatter.8
where the time goes:
time: 806 us; the launch traced here: 804 us
  waiting for transfers between devices  341 us (42%)
  blocking collectives  323 us (40%)
  other arithmetic  48.4 us (6%)
  matrix products  40.3 us (5%)
  local copies, waits for them, and re-layouts  32.3 us (4%)
  between operations  19 us (2%)
    reduce_scatter x1, waiting for transfers between devices, on_device(): lax.psum_scatter(paired[1], 'dp', scatter_dimension=0, tiled=True)  92.4 us
    reduce_scatter x1, waiting for transfers between devices, on_device(): lax.psum_scatter(paired[0], 'dp', scatter_dimension=2, tiled=True)  75.5 us
    reduce_scatter x1, waiting for transfers between devices, on_device(): lax.psum_scatter(paired[2], 'dp', scatter_dimension=0, tiled=True)  73.8 us
    unnamed x8, waiting for transfers between devices  70 us
    all_gather x1, blocking collectives, on_device(): lax.all_gather(w_class.astype(jnp.bfloat16), 'dp', axis=0, tiled=True)  43.3 us
    all_gather x1, blocking collectives, on_device(): lax.all_gather(small_params.astype(jnp.bfloat16), 'dp', axis=1, tiled=True)  43 us
    psum x1, blocking collectives, on_device(): totals_two = lax.psum((shift2_part, gain2_part), ('dp', 'rep'))  41.4 us
    psum x1, blocking collectives, on_device(): grad_norm = jnp.sqrt(lax.psum(local_squares, 'dp'))  40.5 us
  transfers between devices with their start and end apart: 7, of which 6 were waited for; matrix products, arithmetic and copies ran while one was open for 9% of the time, Pallas kernels for 0%

commit v1 on v0

--- a/solution.py
+++ b/solution.py
@@ -6,6 +6,19 @@
 HOPS = 4
 STEP = 7
 EPS_NORM = 1e-05
+
+
+def gather_around(shard, axis, dim):
+    ways = lax.axis_size(axis)
+    up = [(d, (d + 1) % ways) for d in range(ways)]
+    down = [(d, (d - 1) % ways) for d in range(ways)]
+    earlier, later = ([shard], [shard])
+    for _ in range(ways // 2):
+        earlier.append(lax.ppermute(earlier[-1], axis, up))
+    for _ in range((ways - 1) // 2):
+        later.append(lax.ppermute(later[-1], axis, down))
+    line = jnp.concatenate([*earlier[::-1], *later[1:]], axis=dim)
+    return jnp.roll(line, (lax.axis_index(axis) - ways // 2) * shard.shape[dim], axis=dim)
 
 
 def leaky(value, slope):
@@ -68,7 +81,7 @@
     rows = jnp.take(table, batch_index, axis=0)
     input_features = rows.astype(jnp.bfloat16).reshape(batch, HOPS, d_in)
     branch_full, merge_full, class_full, small_full = (
-        lax.all_gather(w_branch.astype(jnp.bfloat16), "dp", axis=2, tiled=True),
+        gather_around(w_branch.astype(jnp.bfloat16), "dp", 2),
         lax.all_gather(w_merge.astype(jnp.bfloat16), "dp", axis=0, tiled=True),
         lax.all_gather(w_class.astype(jnp.bfloat16), "dp", axis=0, tiled=True),
         lax.all_gather(small_params.astype(jnp.bfloat16), "dp", axis=1, tiled=True),

time: 806 us -> 823 us (1.021)
  starting transfers between devices: 0.51 us -> 42.5 us
  waiting for transfers between devices: 341 us -> 312 us
    unnamed x8, waiting for transfers between devices: 70 us -> 25.8 us
    ppermute x0 -> x15, starting transfers between devices: none -> 42.3 us  [the longest x7 42.2 us: gather_around(): later.append(lax.ppermute(later[-1], axis, down))]
    ppermute x0 -> x15, waiting for transfers between devices: none -> 14.5 us  [the longest x8 11.1 us: gather_around(): earlier.append(lax.ppermute(earlier[-1], axis, up))]
  transfers between devices with their start and end apart: 7 -> 22, of which waited for: 6 -> 15; matrix products, arithmetic and copies ran while one was open for 9% -> 9% of each run, Pallas kernels for 0% -> 0%
where the time goes in v1:
time: 823 us; the launch traced here: 821 us
  blocking collectives  327 us (40%)
  waiting for transfers between devices  312 us (38%)
  other arithmetic  43.6 us (5%)
  starting transfers between devices  42.5 us (5%)
  matrix products  38.5 us (5%)
  local copies, waits for them, and re-layouts  38.3 us (5%)
  between operations  19 us (2%)
    reduce_scatter x1, waiting for transfers between devices, on_device(): lax.psum_scatter(paired[1], 'dp', scatter_dimension=0, tiled=True)  92.5 us
    reduce_scatter x1, waiting for transfers between devices, on_device(): lax.psum_scatter(paired[0], 'dp', scatter_dimension=2, tiled=True)  75.5 us
    reduce_scatter x1, waiting for transfers between devices, on_device(): lax.psum_scatter(paired[2], 'dp', scatter_dimension=0, tiled=True)  73.6 us
    all_gather x1, blocking collectives, on_device(): lax.all_gather(w_branch.astype(jnp.bfloat16), 'dp', axis=2, tiled=True)  44.1 us
    ppermute x7, starting transfers between devices, gather_around(): later.append(lax.ppermute(later[-1], axis, down))  42.2 us
    all_gather x1, blocking collectives, on_device(): lax.all_gather(w_class.astype(jnp.bfloat16), 'dp', axis=0, tiled=True)  42 us
    all_gather x1, blocking collectives, on_device(): lax.all_gather(small_params.astype(jnp.bfloat16), 'dp', axis=1, tiled=True)  41.8 us
    psum x1, blocking collectives, on_device(): lax.psum((jnp.sum(pre2, axis=0), jnp.sum(pre2 * pre2, axis=0)), ('dp', 'r...  41 us
  transfers between devices with their start and end apart: 22, of which 15 were waited for; matrix products, arithmetic and copies ran while one was open for 9% of the time, Pallas kernels for 0%

profile of v1, /device:TPU:0, one launch (start us, length us, event | category | flops | bytes accessed | tf_op | source)
XLA Modules:
  0.0 820.9 jit_solution(11482136188271546018)
XLA Ops:
  8.2 7.0 collective-permute-start.8
  17.6 41.8 %all-gather = bf16[16,32,20]{1,2,0:T(8,128)(2,1)S(1)} all-gather(bf16[1,32,20]{1,2,0:T(8,128)(2,1)S(1)} %convert_bitcast_fusion), channel_id=1, replica_groups=mesh['dp'=16,'rep'=2] {'dp'}, dimensions={0}, use_global_device_ids=true | all-gather | bytes 21760 | tf_op jit(solution)/shard_map/all_gather | solution.py:87
  59.6 5.7 collective-permute-start.9
  70.0 6.1 collective-permute-start.10
  78.7 6.1 collective-permute-start.11
  87.1 6.1 collective-permute-start.12
  96.0 5.7 collective-permute-start.13
  104.9 5.6 collective-permute-start.14
  113.8 6.9 copy.57
  120.8 6.7 gather_fusion
  128.2 42.0 %all_gather.16 = bf16[512,47]{1,0:T(8,128)(2,1)S(1)} all-gather(bf16[32,47]{1,0:T(8,128)(2,1)} %convert_element_type.84), channel_id=1, replica_groups=mesh['dp'=16,'rep'=2] {'dp'}, dimensions={0}, use_global_device_ids=true | all-gather | bytes 51136 | tf_op jit(solution)/shard_map/all_gather | solution.py:86
  170.2 5.0 concatenate.12
  175.2 4.8 fusion
  180.1 9.2 %copy.61 = f32[1024,2048]{1,0:T(8,128)} copy(f32[1024,2048]{0,1:T(8,128)} %bitcast.69) | data formatting | bytes 16777216 | tf_op jit(solution)/shard_map/reshape | solution.py:100
  189.2 37.2 %all-reduce.4 = (f32[2048]{0:T(1024)S(1)}, f32[2048]{0:T(1024)S(1)}) all-reduce(f32[2048]{0:T(1024)S(1)} %bitcast.95, f32[2048]{0:T(1024)S(1)} %bitcast.94), channel_id=1, replica_groups=mesh['dp'=16,'rep'=2] {'dp','rep'}, use_global_device_ids=true, to_apply=%region_3.4 | all-reduce | flops 4096 | bytes 32768 | tf_op jit(solution)/shard_map/psum | solution.py:101
  226.4 9.1 %add_convert_fusion = bf16[1024,2048]{1,0:T(8,128)(2,1)} fusion(f32[2048]{0:T(1024)S(1)} %get-tuple-element.89, f32[2048]{0:T(1024)S(1)} %bitcast.84, f32[2048]{0:T(1024)S(1)} %broadcast_subtract_fusion.1, f32[2048]{0:T(1024)S(1)} %bitcast.90, f32[2048]{0:T(1024)S(1)} %get-tuple-element.82, f32[1024,2048]{1,0:T(8,128)} %copy.61, ...), kind=kLoop, calls=%fused_computation.10 | loop fusion | flops 39845888 | bytes 12648448 | tf_op jit(solution)/shard_map/convert_element_type | solution.py:109
  235.6 5.2 multiply_reduce_fusion.5
  240.8 41.0 %all-reduce.3 = (f32[512]{0:T(512)S(1)}, f32[512]{0:T(512)S(1)}) all-reduce(f32[512]{0:T(512)S(1)} %get-tuple-element.40, f32[512]{0:T(512)S(1)} %get-tuple-element.39), channel_id=1, replica_groups=mesh['dp'=16,'rep'=2] {'dp','rep'}, use_global_device_ids=true, to_apply=%region_7.8 | all-reduce | flops 1024 | bytes 8192 | tf_op jit(solution)/shard_map/psum | solution.py:111
  287.5 40.0 %all-reduce.2 = (f32[512]{0:T(512)S(1)}, f32[512]{0:T(512)S(1)}) all-reduce(f32[512]{0:T(512)S(1)} %get-tuple-element.37, f32[512]{0:T(512)S(1)} %get-tuple-element.38), channel_id=1, replica_groups=mesh['dp'=16,'rep'=2] {'dp','rep'}, use_global_device_ids=true, to_apply=%region_13.14 | all-reduce | flops 1024 | bytes 8192 | tf_op jit(solution)/shard_map/psum | solution.py:132
  334.1 13.9 %multiply_reduce_fusion = (bf16[2048]{0:T(1024)(128)(2,1)S(1)}, bf16[2048]{0:T(1024)(128)(2,1)S(1)}, f32[2048]{0:T(1024)S(1)}, f32[2048]{0:T(1024)S(1)}, f32[1024,2048]{1,0:T(8,128)}) fusion(f32[2048]{0:T(1024)S(1)} %broadcast_subtract_fusion.1, f32[2048]{0:T(1024)S(1)} %bitcast.91, f32[2048]{0:T(1024)S(1)} %get-tuple-element.82, ...), kind=kOutput, calls=%fused_computation.4 | convolution fusion | flops 2225070080 | bytes 20013056 | tf_op jit(solution)/shard_map/dot_general | solution.py:42
  348.1 40.4 %all-reduce.1 = (f32[2048]{0:T(1024)S(1)}, f32[2048]{0:T(1024)S(1)}) all-reduce(f32[2048]{0:T(1024)S(1)} %get-tuple-element.32, f32[2048]{0:T(1024)S(1)} %get-tuple-element.33), channel_id=1, replica_groups=mesh['dp'=16,'rep'=2] {'dp','rep'}, use_global_device_ids=true, to_apply=%region_17.18 | all-reduce | flops 4096 | bytes 32768 | tf_op jit(solution)/shard_map/psum | solution.py:147
  390.5 7.2 multiply_convert_fusion
  402.2 6.7 all-reduce.10.cloned.1.call-done
  412.3 23.1 %all-reduce.12.cloned.1.call-done = (bf16[4,100,512]{1,2,0:T(8,128)(2,1)}, bf16[2048,512]{1,0:T(8,128)(2,1)}) async-done(((bf16[4,100,512]{1,2,0:T(8,128)(2,1)}, bf16[2048,512]{1,0:T(8,128)(2,1)}), (bf16[4,100,512]{1,2,0:T(8,128)(2,1)}, bf16[2048,512]{1,0:T(8,128)(2,1)})) %all-reduce.12.cloned.1.call-update) | async-done | bytes 2506768 | tf_op jit(solution)/shard_map/psum | solution.py:178
  437.6 4.2 convert_element_type.92
  441.9 44.1 %all_gather.17 = bf16[4,100,512]{1,0,2:T(4,128)(2,1)S(1)} all-gather(bf16[4,100,32]{1,0,2:T(4,128)(2,1)S(1)} %copy.63), channel_id=1, replica_groups=mesh['dp'=16,'rep'=2] {'dp'}, dimensions={2}, use_global_device_ids=true | all-gather | bytes 435200 | tf_op jit(solution)/shard_map/all_gather | solution.py:122
  486.1 3.7 fusion.7
  489.8 25.7 %reduce-scatter.13.cloned.1.call-done = f32[32,20]{1,0:T(8,128)} async-done(((f32[512,20]{1,0:T(8,128)}), f32[32,20]{1,0:T(8,128)}) %reduce-scatter.13.cloned.1.call-update) | async-done | bytes 2576
  517.0 73.6 %reduce-scatter.11.cloned.1.call-done = f32[32,47]{1,0:T(8,128)} async-done(((f32[512,47]{1,0:T(8,128)}), f32[32,47]{1,0:T(8,128)}) %reduce-scatter.11.cloned.1.call-update) | async-done | bytes 6032 | tf_op jit(solution)/shard_map/reduce_scatter | solution.py:186
  591.9 75.5 %reduce-scatter.7.cloned.1.call-done = f32[4,100,32]{1,2,0:T(8,128)} async-done(((f32[4,100,512]{1,2,0:T(8,128)}), f32[4,100,32]{1,2,0:T(8,128)}) %reduce-scatter.7.cloned.1.call-update) | async-done | bytes 51216 | tf_op jit(solution)/shard_map/reduce_scatter | solution.py:184
  668.9 92.5 %reduce-scatter.9.cloned.1.call-done = f32[128,512]{1,0:T(8,128)} async-done(((f32[2048,512]{1,0:T(8,128)}), f32[128,512]{1,0:T(8,128)}) %reduce-scatter.9.cloned.1.call-update) | async-done | bytes 262160 | tf_op jit(solution)/shard_map/reduce_scatter | solution.py:185
  767.0 40.6 %psum.103 = f32[]{:T(128)} all-reduce(f32[]{:T(128)S(6)} %add.247), channel_id=1, replica_groups=mesh['dp'=16,'rep'=2] {'dp'}, use_global_device_ids=true, to_apply=%region_34.35 | all-reduce | flops 1 | bytes 8 | tf_op jit(solution)/shard_map/psum | solution.py:192
  (159 shorter events, 59.4 us)
Async XLA Ops:
  7.2 228.4 %all-gather.3.cloned.1.call-start = ((), (), s32[]{:S(2)}) async-start(), calls=%async_computation.4 | async-start | bytes 2228224 | tf_op jit(solution)/shard_map/all_gather | solution.py:85
  8.2 51.3 %collective-permute-start.8 = (bf16[4,100,32]{2,1,0:T(8,128)(2,1)S(1)}, bf16[4,100,32]{2,1,0:T(8,128)(2,1)S(1)}, u32[]{:S(2)}, u32[]{:S(2)}) collective-permute-start(bf16[4,100,32]{2,1,0:T(8,128)(2,1)S(1)} %copy.59), channel_id=1, source_target_pairs={{0,30},{2,0},{4,2},{6,4},{8,6},{10,8},{12,10},{14,12},{16,14},{18,... | collective-permute-start | bytes 76808 | tf_op jit(solution)/shard_map/ppermute | solution.py:19
  15.2 44.2 %collective-permute-start = (bf16[4,100,32]{2,1,0:T(8,128)(2,1)S(1)}, bf16[4,100,32]{2,1,0:T(8,128)(2,1)S(1)}, u32[]{:S(2)}, u32[]{:S(2)}) collective-permute-start(bf16[4,100,32]{2,1,0:T(8,128)(2,1)S(1)} %copy.59), channel_id=1, source_target_pairs={{0,2},{2,4},{4,6},{6,8},{8,10},{10,12},{12,14},{14,16},{16,18},{18... | collective-permute-start | bytes 76808 | tf_op jit(solution)/shard_map/ppermute | solution.py:17
  16.9 392.1 %all-reduce.10.cloned.1.call-start = ((), (), s32[]{:S(2)}) async-start(), calls=%async_computation.9 | async-start | bytes 311296 | tf_op jit(solution)/shard_map/psum | solution.py:180
  59.4 8.5 %collective-permute-start.1 = (bf16[4,100,32]{2,1,0:T(8,128)(2,1)S(1)}, bf16[4,100,32]{2,1,0:T(8,128)(2,1)S(1)}, u32[]{:S(2)}, u32[]{:S(2)}) collective-permute-start(bf16[4,100,32]{2,1,0:T(8,128)(2,1)S(1)} %collective-permute-done), channel_id=1, source_target_pairs={{0,2},{2,4},{4,6},{6,8},{8,10},{10,12},{12,14},{14,16},{16,18},{18... | collective-permute-start | bytes 76808 | tf_op jit(solution)/shard_map/ppermute | solution.py:17
  59.6 10.4 %collective-permute-start.9 = (bf16[4,100,32]{2,1,0:T(8,128)(2,1)S(1)}, bf16[4,100,32]{2,1,0:T(8,128)(2,1)S(1)}, u32[]{:S(2)}, u32[]{:S(2)}) collective-permute-start(bf16[4,100,32]{2,1,0:T(8,128)(2,1)S(1)} %collective-permute-done.8), channel_id=1, source_target_pairs={{0,30},{2,0},{4,2},{6,4},{8,6},{10,8},{12,10},{14,12},{16,14},{18,... | collective-permute-start | bytes 76808 | tf_op jit(solution)/shard_map/ppermute | solution.py:19
  67.9 9.0 %collective-permute-start.2 = (bf16[4,100,32]{2,1,0:T(8,128)(2,1)S(1)}, bf16[4,100,32]{2,1,0:T(8,128)(2,1)S(1)}, u32[]{:S(2)}, u32[]{:S(2)}) collective-permute-start(bf16[4,100,32]{2,1,0:T(8,128)(2,1)S(1)} %collective-permute-done.1), channel_id=1, source_target_pairs={{0,2},{2,4},{4,6},{6,8},{8,10},{10,12},{12,14},{14,16},{16,18},{18... | collective-permute-start | bytes 76808 | tf_op jit(solution)/shard_map/ppermute | solution.py:17
  70.0 8.7 %collective-permute-start.10 = (bf16[4,100,32]{2,1,0:T(8,128)(2,1)S(1)}, bf16[4,100,32]{2,1,0:T(8,128)(2,1)S(1)}, u32[]{:S(2)}, u32[]{:S(2)}) collective-permute-start(bf16[4,100,32]{2,1,0:T(8,128)(2,1)S(1)} %collective-permute-done.9), channel_id=1, source_target_pairs={{0,30},{2,0},{4,2},{6,4},{8,6},{10,8},{12,10},{14,12},{16,14},{18,... | collective-permute-start | bytes 76808 | tf_op jit(solution)/shard_map/ppermute | solution.py:19
  76.9 10.1 %collective-permute-start.3 = (bf16[4,100,32]{2,1,0:T(8,128)(2,1)S(1)}, bf16[4,100,32]{2,1,0:T(8,128)(2,1)S(1)}, u32[]{:S(2)}, u32[]{:S(2)}) collective-permute-start(bf16[4,100,32]{2,1,0:T(8,128)(2,1)S(1)} %collective-permute-done.2), channel_id=1, source_target_pairs={{0,2},{2,4},{4,6},{6,8},{8,10},{10,12},{12,14},{14,16},{16,18},{18... | collective-permute-start | bytes 76808 | tf_op jit(solution)/shard_map/ppermute | solution.py:17
  78.7 8.4 %collective-permute-start.11 = (bf16[4,100,32]{2,1,0:T(8,128)(2,1)S(1)}, bf16[4,100,32]{2,1,0:T(8,128)(2,1)S(1)}, u32[]{:S(2)}, u32[]{:S(2)}) collective-permute-start(bf16[4,100,32]{2,1,0:T(8,128)(2,1)S(1)} %collective-permute-done.10), channel_id=1, source_target_pairs={{0,30},{2,0},{4,2},{6,4},{8,6},{10,8},{12,10},{14,12},{16,14},{18,... | collective-permute-start | bytes 76808 | tf_op jit(solution)/shard_map/ppermute | solution.py:19
  87.0 8.3 %collective-permute-start.4 = (bf16[4,100,32]{2,1,0:T(8,128)(2,1)S(1)}, bf16[4,100,32]{2,1,0:T(8,128)(2,1)S(1)}, u32[]{:S(2)}, u32[]{:S(2)}) collective-permute-start(bf16[4,100,32]{2,1,0:T(8,128)(2,1)S(1)} %collective-permute-done.3), channel_id=1, source_target_pairs={{0,2},{2,4},{4,6},{6,8},{8,10},{10,12},{12,14},{14,16},{16,18},{18... | collective-permute-start | bytes 76808 | tf_op jit(solution)/shard_map/ppermute | solution.py:17
  87.1 8.9 %collective-permute-start.12 = (bf16[4,100,32]{2,1,0:T(8,128)(2,1)S(1)}, bf16[4,100,32]{2,1,0:T(8,128)(2,1)S(1)}, u32[]{:S(2)}, u32[]{:S(2)}) collective-permute-start(bf16[4,100,32]{2,1,0:T(8,128)(2,1)S(1)} %collective-permute-done.11), channel_id=1, source_target_pairs={{0,30},{2,0},{4,2},{6,4},{8,6},{10,8},{12,10},{14,12},{16,14},{18,... | collective-permute-start | bytes 76808 | tf_op jit(solution)/shard_map/ppermute | solution.py:19
  95.3 8.3 %collective-permute-start.5 = (bf16[4,100,32]{2,1,0:T(8,128)(2,1)S(1)}, bf16[4,100,32]{2,1,0:T(8,128)(2,1)S(1)}, u32[]{:S(2)}, u32[]{:S(2)}) collective-permute-start(bf16[4,100,32]{2,1,0:T(8,128)(2,1)S(1)} %collective-permute-done.4), channel_id=1, source_target_pairs={{0,2},{2,4},{4,6},{6,8},{8,10},{10,12},{12,14},{14,16},{16,18},{18... | collective-permute-start | bytes 76808 | tf_op jit(solution)/shard_map/ppermute | solution.py:17
  96.0 8.9 %collective-permute-start.13 = (bf16[4,100,32]{2,1,0:T(8,128)(2,1)S(1)}, bf16[4,100,32]{2,1,0:T(8,128)(2,1)}, u32[]{:S(2)}, u32[]{:S(2)}) collective-permute-start(bf16[4,100,32]{2,1,0:T(8,128)(2,1)S(1)} %collective-permute-done.12), channel_id=1, source_target_pairs={{0,30},{2,0},{4,2},{6,4},{8,6},{10,8},{12,10},{14,12},{16,14},{18,... | collective-permute-start | bytes 76808 | tf_op jit(solution)/shard_map/ppermute | solution.py:19
  103.6 8.4 %collective-permute-start.6 = (bf16[4,100,32]{2,1,0:T(8,128)(2,1)S(1)}, bf16[4,100,32]{2,1,0:T(8,128)(2,1)}, u32[]{:S(2)}, u32[]{:S(2)}) collective-permute-start(bf16[4,100,32]{2,1,0:T(8,128)(2,1)S(1)} %collective-permute-done.5), channel_id=1, source_target_pairs={{0,2},{2,4},{4,6},{6,8},{8,10},{10,12},{12,14},{14,16},{16,18},{18... | collective-permute-start | bytes 76808 | tf_op jit(solution)/shard_map/ppermute | solution.py:17
  104.9 65.3 %collective-permute-start.14 = (bf16[4,100,32]{2,1,0:T(8,128)(2,1)}, bf16[4,100,32]{2,1,0:T(8,128)(2,1)}, u32[]{:S(2)}, u32[]{:S(2)}) collective-permute-start(bf16[4,100,32]{2,1,0:T(8,128)(2,1)} %collective-permute-done.13), channel_id=1, source_target_pairs={{0,30},{2,0},{4,2},{6,4},{8,6},{10,8},{12,10},{14,12},{16,14},{18,... | collective-permute-start | bytes 76808 | tf_op jit(solution)/shard_map/ppermute | solution.py:19
  112.0 58.2 %collective-permute-start.7 = (bf16[4,100,32]{2,1,0:T(8,128)(2,1)}, bf16[4,100,32]{2,1,0:T(8,128)(2,1)}, u32[]{:S(2)}, u32[]{:S(2)}) collective-permute-start(bf16[4,100,32]{2,1,0:T(8,128)(2,1)} %collective-permute-done.6), channel_id=1, source_target_pairs={{0,2},{2,4},{4,6},{6,8},{8,10},{10,12},{12,14},{14,16},{16,18},{18... | collective-permute-start | bytes 76808 | tf_op jit(solution)/shard_map/ppermute | solution.py:17
  390.5 45.0 %all-reduce.12.cloned.1.call-start = ((), (), s32[]{:S(2)}) async-start(), calls=%async_computation.10 | async-start | bytes 5242880 | tf_op jit(solution)/shard_map/psum | solution.py:178
  402.2 113.4 %reduce-scatter.13.cloned.1.call-start = ((), (), s32[]{:S(2)}) async-start(), calls=%async_computation.8 | async-start | bytes 278528
  410.6 180.0 %reduce-scatter.11.cloned.1.call-start = ((), (), s32[]{:S(2)}) async-start(), calls=%async_computation.7 | async-start | bytes 278528 | tf_op jit(solution)/shard_map/reduce_scatter | solution.py:186
  412.3 255.1 %reduce-scatter.7.cloned.1.call-start = ((), (), s32[]{:S(2)}) async-start(), calls=%async_computation.5 | async-start | bytes 1114112 | tf_op jit(solution)/shard_map/reduce_scatter | solution.py:184
  437.6 323.8 %reduce-scatter.9.cloned.1.call-start = ((), (), s32[]{:S(2)}) async-start(), calls=%async_computation.6 | async-start | bytes 4456448 | tf_op jit(solution)/shard_map/reduce_scatter | solution.py:185
  486.0 322.3 %copy-start.20 = (f32[20,32]{1,0:T(8,128)S(1)}, f32[20,32]{1,0:T(8,128)}, u32[]{:S(2)}) copy-start(f32[20,32]{1,0:T(8,128)} %param.31) | copy-start | bytes 7684
  486.0 323.0 %copy-start.15 = (f32[32,47]{1,0:T(8,128)S(1)}, f32[32,47]{1,0:T(8,128)}, u32[]{:S(2)}) copy-start(f32[32,47]{1,0:T(8,128)} %param.22) | copy-start | bytes 18052
  486.0 323.0 %copy-start.17 = (f32[32,47]{1,0:T(8,128)S(1)}, f32[32,47]{1,0:T(8,128)}, u32[]{:S(2)}) copy-start(f32[32,47]{1,0:T(8,128)} %param.26) | copy-start | bytes 18052
  486.0 323.0 %copy-start.18 = (f32[32,47]{1,0:T(8,128)S(1)}, f32[32,47]{1,0:T(8,128)}, u32[]{:S(2)}) copy-start(f32[32,47]{1,0:T(8,128)} %param.30) | copy-start | bytes 18052
  486.0 324.3 %copy-start.12 = (f32[4,100,32]{1,2,0:T(8,128)S(1)}, f32[4,100,32]{1,2,0:T(8,128)}, u32[]{:S(2)}) copy-start(f32[4,100,32]{1,2,0:T(8,128)} %param.20) | copy-start | bytes 153604
  486.0 324.3 %copy-start.13 = (f32[4,100,32]{1,2,0:T(8,128)S(1)}, f32[4,100,32]{1,2,0:T(8,128)}, u32[]{:S(2)}) copy-start(f32[4,100,32]{1,2,0:T(8,128)} %param.24) | copy-start | bytes 153604
  486.0 324.3 %copy-start.14 = (f32[4,100,32]{1,2,0:T(8,128)S(1)}, f32[4,100,32]{1,2,0:T(8,128)}, u32[]{:S(2)}) copy-start(f32[4,100,32]{1,2,0:T(8,128)} %param.28) | copy-start | bytes 153604
  486.0 325.8 %copy-start.2 = (f32[128,512]{1,0:T(8,128)S(1)}, f32[128,512]{1,0:T(8,128)}, u32[]{:S(2)}) copy-start(f32[128,512]{1,0:T(8,128)} %param.21) | copy-start | bytes 786436
  486.1 325.8 %copy-start.10 = (f32[128,512]{1,0:T(8,128)S(1)}, f32[128,512]{1,0:T(8,128)}, u32[]{:S(2)}) copy-start(f32[128,512]{1,0:T(8,128)} %param.25) | copy-start | bytes 786436
  486.1 325.8 %copy-start.11 = (f32[128,512]{1,0:T(8,128)S(1)}, f32[128,512]{1,0:T(8,128)}, u32[]{:S(2)}) copy-start(f32[128,512]{1,0:T(8,128)} %param.29) | copy-start | bytes 786436
  (20 other events, 1130.0 us)
Sparse Core Ops, SparseCore 0:
  17.0 70.6 all-gather.2
  390.6 18.3 all-reduce.9
  412.0 23.4 all-reduce.11
  438.2 77.2 reduce-scatter.12
  518.2 72.3 reduce-scatter.10
  593.4 74.0 reduce-scatter.6
  669.7 91.6 reduce-scatter.8
